TPU v7x, 256 devices: a whole 4x4x8 slice. The times are simulated.
256 devices in a mesh: dp: 2 (over core), ctx: 128 (over y, z, x).
Axes of the slice: x: 4, y: 4, z: 8, core: 2. Of those that a mesh axis runs over, the one named last changes fastest.
Arguments:
- queries: bfloat16 [32768, 1024], P(('dp', 'ctx')), parts along dimension 0, may hold values from -6 to 6
- keys: bfloat16 [32768, 1024], P(('dp', 'ctx')), parts along dimension 0, may hold values from -6 to 6
- values: bfloat16 [32768, 1024], P(('dp', 'ctx')), parts along dimension 0, may hold values from -7.5 to 7.5
- hidden: bfloat16 [32768, 1024], P(('dp', 'ctx')), parts along dimension 0, may hold values from -60 to 60
- out_weight: bfloat16 [1024, 1024], replicated, may hold values from -0.1875 to 0.1875
- norm_gain: float32 [1024], replicated, may hold values from 0.1 to 1.9
- random_blocks: int32 [512, 16, 3], P('dp'), parts along dimension 0, may hold values from 0 to 255, as said below
- global_blocks: int32 [4], P('dp'), parts along dimension 0, may hold values from 0 to 255, as said below
Outputs:
- normed: bfloat16 [32768, 1024], P(('dp', 'ctx')), parts along dimension 0
There are 2 independent parts, one for each index of `dp`. A program takes and returns all parts, laid end to end along the dimension named above; an argument that names none is the same for every part. Nothing has to cross between parts.
Inputs may be any that keep to these rules, and one draw needn't show every extreme that they name: `random_blocks`: among the random blocks named by the query blocks of one index of ctx (rows d * 2 to (d + 1) * 2 - 1, all heads), at most 2 lie in the blocks of any one index of ctx (block // 2); for every d some index is named exactly 2 times. `global_blocks`: the 2 global blocks are distinct, and one of them is the last block of the document.
All inputs are finite; a program needn't handle non-finite values.
Results may differ from a plain program's by a relative error of at most 0.001.
The roundings to bfloat16 on the way count: a program that leaves them out, or rounds other values in their place, can miss the bound.
Values may be sent and summed in bfloat16 or wider, within the bound.
A program may use at most 64 MiB of HBM per device.

v0:
```python
import math

import jax
import jax.numpy as jnp
from jax import lax
from jax.sharding import PartitionSpec as P

H = 16
BLOCK = 64
R = 3
G = 2
REACH = 1


def padded_2(block, sides, width):
    for axis, dim in sides:
        count = lax.axis_size(axis)
        forward = [(i, i + 1) for i in range(count - 1)]
        backward = [(target, source) for source, target in forward]
        low = lax.ppermute(
            lax.slice_in_dim(block, block.shape[dim] - width, None, axis=dim), axis, forward
        )
        high = lax.ppermute(lax.slice_in_dim(block, 0, width, axis=dim), axis, backward)
        block = jnp.concatenate([low, block, high], axis=dim)
    return block


def from_root(block, axis, source):
    block = jnp.where(lax.axis_index(axis) == source, block, jnp.zeros_like(block))
    return lax.psum(block, axis)


def per_device(queries, keys, values, hidden, out_weight, norm_gain, random_blocks, global_blocks):
    row_count, model_width = queries.shape
    head_count = H
    head_size = model_width // head_count
    block_count = row_count // BLOCK
    device_count = lax.axis_size("ctx")
    my_index = lax.axis_index("ctx")
    total_blocks = block_count * device_count
    score_scale = 1.0 / math.sqrt(head_size)
    window_span = 2 * REACH + 1
    request_count = block_count * head_count * R
    capacity = (request_count + device_count - 1) // device_count + 1
    key_heads = keys.reshape(row_count, head_count, head_size)
    value_heads = values.reshape(row_count, head_count, head_size)
    kv_rows = jnp.concatenate([key_heads, value_heads], axis=2)
    kv_blocks = kv_rows.reshape(block_count, BLOCK, head_count, 2 * head_size)
    query_blocks = queries.reshape(block_count, BLOCK, head_count, head_size)
    padded = padded_2(
        kv_rows.reshape(row_count, head_count * 2 * head_size), (("ctx", 0),), REACH * BLOCK
    )
    padded = padded.reshape(block_count + 2 * REACH, BLOCK, head_count, 2 * head_size)
    owner_of_global = global_blocks // block_count
    local_of_global = global_blocks - owner_of_global * block_count

    def own_rows(global_slot):
        query_part = lax.dynamic_slice_in_dim(query_blocks, local_of_global[global_slot], 1, 0)[0]
        kv_part = lax.dynamic_slice_in_dim(kv_blocks, local_of_global[global_slot], 1, 0)[0]
        return jnp.concatenate([query_part, kv_part], axis=2).reshape(
            BLOCK, head_count * 3 * head_size
        )

    shared = jnp.stack(
        [
            from_root(own_rows(global_slot), "ctx", owner_of_global[global_slot])
            for global_slot in range(G)
        ],
        axis=0,
    )
    shared = shared.reshape(G * BLOCK, head_count, 3 * head_size)
    global_queries = shared[..., :head_size]
    global_kv = shared[..., head_size:]
    request_heads = jnp.arange(request_count, dtype=jnp.int32) // R % head_count
    my_requests = lax.dynamic_slice_in_dim(
        random_blocks, my_index * block_count, block_count, 0
    ).reshape(request_count)
    every_request = random_blocks.reshape(device_count, request_count)
    owners = every_request // block_count
    mine_mask = owners == my_index
    rank_in = jnp.cumsum(mine_mask.astype(jnp.int32), axis=1) - 1
    slot_index = jnp.arange(capacity, dtype=jnp.int32)
    slot_match = mine_mask[:, :, None] & (rank_in[:, :, None] == slot_index[None, None, :])
    which_block = jnp.sum(
        jnp.where(slot_match, (every_request % block_count)[:, :, None], 0), axis=1
    )
    which_head = jnp.sum(jnp.where(slot_match, request_heads[None, :, None], 0), axis=1)
    payload = kv_blocks[which_block, :, which_head, :]
    received = lax.all_to_all(payload, "ctx", split_axis=0, concat_axis=0, tiled=True)
    my_owners = my_requests // block_count
    owner_match = my_owners[:, None] == jnp.arange(device_count, dtype=jnp.int32)[None, :]
    running = jnp.cumsum(owner_match.astype(jnp.int32), axis=0)
    my_rank = jnp.sum(jnp.where(owner_match, running, 0), axis=1) - 1
    tile_rows = received[my_owners, my_rank]
    tile_rows = tile_rows.reshape(block_count, head_count, R, BLOCK, 2 * head_size)
    group_size = math.gcd(block_count, max(1, 512 // BLOCK))
    offsets = jnp.arange(window_span, dtype=jnp.int32) - REACH

    def group_context(block_start):
        window = jnp.stack(
            [
                lax.dynamic_slice_in_dim(padded, block_start + shift_index, group_size, 0)
                for shift_index in range(window_span)
            ],
            axis=1,
        )
        target = (
            my_index * block_count
            + block_start
            + jnp.arange(group_size, dtype=jnp.int32)[:, None]
            + offsets[None, :]
        )
        allowed = (target >= 0) & (target < total_blocks)
        s_window = (
            jnp.einsum(
                "bqhd,bwkhd->bhqwk",
                query_blocks,
                window[..., :head_size],
                preferred_element_type=jnp.float32,
            )
            * score_scale
        )
        s_window = jnp.where(allowed[:, None, None, :, None], s_window, -1e30)
        s_global = (
            jnp.einsum(
                "bqhd,khd->bhqk",
                query_blocks,
                global_kv[..., :head_size],
                preferred_element_type=jnp.float32,
            )
            * score_scale
        )
        s_random = (
            jnp.einsum(
                "bqhd,bhrkd->bhqrk",
                query_blocks,
                tile_rows[..., :head_size],
                preferred_element_type=jnp.float32,
            )
            * score_scale
        )
        all_scores = jnp.concatenate(
            [
                s_window.reshape(group_size, head_count, BLOCK, window_span * BLOCK),
                s_global,
                s_random.reshape(group_size, head_count, BLOCK, R * BLOCK),
            ],
            axis=3,
        )
        probabilities = jax.nn.softmax(all_scores, axis=3).astype(jnp.bfloat16)
        window_probs = probabilities[..., : window_span * BLOCK].reshape(
            group_size, head_count, BLOCK, window_span, BLOCK
        )
        global_probs = probabilities[..., window_span * BLOCK : (window_span + G) * BLOCK]
        random_probs = probabilities[..., (window_span + G) * BLOCK :].reshape(
            group_size, head_count, BLOCK, R, BLOCK
        )
        context_part = jnp.einsum(
            "bhqwk,bwkhd->bqhd",
            window_probs,
            window[..., head_size:],
            preferred_element_type=jnp.float32,
        )
        context_part = context_part + jnp.einsum(
            "bhqk,khd->bqhd",
            global_probs,
            global_kv[..., head_size:],
            preferred_element_type=jnp.float32,
        )
        context_part = context_part + jnp.einsum(
            "bhqrk,bhrkd->bqhd",
            random_probs,
            tile_rows[..., head_size:],
            preferred_element_type=jnp.float32,
        )
        return context_part

    starts = jnp.arange(block_count // group_size, dtype=jnp.int32) * group_size
    context = lax.map(group_context, starts).reshape(block_count, BLOCK, head_count, head_size)
    scores_global = (
        jnp.einsum("qhd,khd->hqk", global_queries, key_heads, preferred_element_type=jnp.float32)
        * score_scale
    )
    local_peak = jnp.max(scores_global, axis=2)
    value_wide = value_heads.astype(jnp.float32)
    peak_score = lax.pmax(local_peak, "ctx")
    weights = jnp.exp(scores_global - peak_score[..., None])
    local_numer = jnp.einsum("hqk,khd->hqd", weights, value_wide, precision=lax.Precision.HIGHEST)
    totals, numerators = lax.psum((jnp.sum(weights, axis=2), local_numer), "ctx")
    global_context = numerators / totals[..., None]
    global_context = jnp.transpose(global_context, (1, 0, 2)).reshape(
        G, BLOCK, head_count, head_size
    )
    block_ids = my_index * block_count + jnp.arange(block_count, dtype=jnp.int32)
    for global_slot in range(G):
        is_global = (block_ids == global_blocks[global_slot])[:, None, None, None]
        context = jnp.where(is_global, global_context[global_slot][None], context)
    attended = context.reshape(row_count, model_width).astype(jnp.bfloat16)
    mixed_rows = hidden.astype(jnp.float32) + jnp.dot(
        attended, out_weight, preferred_element_type=jnp.float32
    )
    row_mean = jnp.mean(mixed_rows, axis=1, keepdims=True)
    centred = mixed_rows - row_mean
    variance = jnp.mean(centred * centred, axis=1, keepdims=True)
    return (centred * lax.rsqrt(variance + 1e-05) * norm_gain[None, :]).astype(jnp.bfloat16)


def solution(mesh):
    placed = (
        P(("dp", "ctx"), None),
        P(("dp", "ctx"), None),
        P(("dp", "ctx"), None),
        P(("dp", "ctx"), None),
        P(),
        P(),
        P("dp", None, None),
        P("dp"),
    )
    return jax.shard_map(
        per_device, mesh=mesh, in_specs=placed, out_specs=P(("dp", "ctx"), None), check_vma=False
    )
```

profile of v0, /device:TPU:6, one launch (start us, length us, event | category | flops | bytes accessed | tf_op | source)
XLA Modules:
  0.0 1063.2 jit_solution(2555190714936128930)
XLA Ops:
  6.5 1.5 concatenate.40
  8.2 1.3 concatenate.41
  9.5 1.0 copy.205
  10.5 2.4 copy.225
  12.9 3.2 reshape.404
  17.2 1.3 pad_maximum_fusion.5
  18.6 3.4 gather_fusion
  21.9 15.8 %all-to-all-start = ((bf16[128,2,64,128]{3,2,1,0:T(8,128)(2,1)}), bf16[128,2,64,128]{3,2,1,0:T(8,128)(2,1)}, u32[]{:S(2)}, u32[]{:S(2)}) async-start(bf16[128,2,64,128]{3,2,1,0:T(8,128)(2,1)} %bitcast.112), calls=%async_computation | async-start | bytes 8388608 | tf_op jit(solution)/shard_map/all_to_all | solution.py:89
  37.8 1.2 copy.210
  39.0 1.8 copy.209
  40.8 2.3 fusion.18
  43.1 1.9 copy.214
  45.0 3.4 collective-permute-start
  48.4 1.9 copy.218
  50.3 2.5 collective-permute-start.1
  57.3 1.0 fusion.29
  58.3 0.9 copy.287
  59.2 1.3 reshape.398
  61.9 2.0 maximum_select_fusion.1
  63.9 2.5 stack.24
  67.9 2.1 maximum_select_fusion
  70.0 2.4 stack.23
  73.6 1.3 broadcast_compare_fusion
  75.1 0.9 pad_maximum_fusion.2
  76.0 1.2 concatenate.48
  77.2 2.2 concatenate.47
  79.4 0.9 copy.224
  80.3 1.1 copy.215
  81.4 1.2 copy.217
  82.6 2.0 copy.216
  85.0 50.7 %collective-permute-done = bf16[64,2048]{1,0:T(8,128)(2,1)} collective-permute-done((bf16[64,2048]{1,0:T(8,128)(2,1)}, bf16[64,2048]{1,0:T(8,128)(2,1)}, u32[]{:S(2)}, u32[]{:S(2)}) %collective-permute-start) | collective-permute-done | bytes 262176 | tf_op jit(solution)/shard_map/ppermute | solution.py:20
  135.7 2.2 collective-permute-done.1
  137.9 1.3 fusion.22
  140.6 2.5 bitcast_reduce_fusion.1
  143.1 3.6 copy.234
  146.7 154.0 %all-reduce.6.cloned.1.call-done = (bf16[1,64,3072]{2,1,0:T(8,128)(2,1)}, bf16[1,64,3072]{2,1,0:T(8,128)(2,1)}) async-done(((bf16[1,64,3072]{2,1,0:T(8,128)(2,1)}, bf16[1,64,3072]{2,1,0:T(8,128)(2,1)}), (bf16[1,64,3072]{2,1,0:T(8,128)(2,1)}, bf16[1,64,3072]{2,1,0:T(8,128)(2,1)})) %all-reduce.6.cloned.1.call-update) | async-done | bytes 786448 | tf_op jit(solution)/shard_map/psum | solution.py:30
  300.7 2.1 pad_maximum_fusion.1
  302.8 2.2 reshape.399
  305.1 1.3 fusion.55
  306.9 340.9 %pmax.7 = f32[16,128]{1,0:T(8,128)S(1)} all-reduce(f32[16,128]{1,0:T(8,128)S(1)} %get-tuple-element.58), channel_id=1, replica_groups=mesh['dp'=2,'ctx'=128] {'ctx'}, use_global_device_ids=true, to_apply=%region_3.4 | all-reduce | flops 2048 | bytes 16384 | tf_op jit(solution)/shard_map/pmax | solution.py:186
  647.9 1.5 fusion.17
  649.4 2.1 copy.261
  651.6 1.8 fusion.23
  653.5 351.2 %psum.31 = f32[16,128]{1,0:T(8,128)S(1)} all-reduce(f32[16,128]{1,0:T(8,128)S(1)} %fusion.16), channel_id=1, replica_groups=mesh['dp'=2,'ctx'=128] {'ctx'}, use_global_device_ids=true, to_apply=%region_6.7 | all-reduce | flops 2048 | bytes 16384 | tf_op jit(solution)/shard_map/psum | solution.py:189
  1005.1 1.2 multiply_bitcast_fusion
  1006.3 1.1 divide_bitcast_fusion
  1008.2 1.2 copy.212
  1010.3 1.4 broadcast_in_dim.116
  1011.8 1.9 copy.213
  1013.6 1.8 broadcast_in_dim.120
  1015.4 2.1 broadcast_in_dim.121
  1017.6 4.6 gather_fusion.1
  1022.2 3.8 bitcast_reduce_fusion
  1026.0 3.6 copy.236
  1029.6 4.4 fusion.1
  1034.0 2.7 divide_convert_fusion
  1036.7 1.7 fusion.54
  1038.4 1.6 copy.242
  1039.9 3.3 fusion.11
  1043.2 2.5 copy.238
  1045.8 3.3 fusion.8
  1049.1 2.8 fusion.15
  1051.9 1.5 copy.245
  1053.7 1.6 fusion.61
  (90 shorter events, 11.0 us)
Async XLA Ops:
  6.5 1047.1 %copy-start = (bf16[1024,1024]{1,0:T(8,128)(2,1)S(1)}, bf16[1024,1024]{1,0:T(8,128)(2,1)}, u32[]{:S(2)}) copy-start(bf16[1024,1024]{1,0:T(8,128)(2,1)} %param.12) | copy-start | bytes 6291460
  6.5 4.0 copy-start.16
  21.9 995.7 %all-to-all-start = ((bf16[128,2,64,128]{3,2,1,0:T(8,128)(2,1)}), bf16[128,2,64,128]{3,2,1,0:T(8,128)(2,1)}, u32[]{:S(2)}, u32[]{:S(2)}) async-start(bf16[128,2,64,128]{3,2,1,0:T(8,128)(2,1)} %bitcast.112), calls=%async_computation | async-start | bytes 8388608 | tf_op jit(solution)/shard_map/all_to_all | solution.py:89
  37.8 15.0 %copy-start.18 = (s32[2]{0:T(128)S(1)}, s32[2]{0:T(128)}, u32[]{:S(2)}) copy-start(s32[2]{0:T(128)} %param.15) | copy-start | bytes 28
  37.8 19.5 %copy-start.8 = (bf16[2,64,16,64]{3,1,2,0:T(8,128)(2,1)S(1)}, bf16[2,64,16,64]{3,1,2,0:T(8,128)(2,1)}, u32[]{:S(2)}) copy-start(bf16[2,64,16,64]{3,1,2,0:T(8,128)(2,1)} %copy.205) | copy-start | bytes 786436
  37.8 262.9 %all-reduce.6.cloned.1.call-start = ((), (), s32[]{:S(2)}) async-start(), calls=%async_computation.2 | async-start | bytes 1572864 | tf_op jit(solution)/shard_map/psum | solution.py:30
  45.0 90.7 %collective-permute-start = (bf16[64,2048]{1,0:T(8,128)(2,1)}, bf16[64,2048]{1,0:T(8,128)(2,1)}, u32[]{:S(2)}, u32[]{:S(2)}) collective-permute-start(bf16[64,2048]{1,0:T(8,128)(2,1)} %copy.214), channel_id=1, source_target_pairs={{0,1},{1,2},{2,3},{3,4},{4,5},{5,6},{6,7},{7,8},{8,9},{9,10},{10,1... | collective-permute-start | bytes 786440 | tf_op jit(solution)/shard_map/ppermute | solution.py:20
  50.3 87.5 %collective-permute-start.1 = (bf16[64,2048]{1,0:T(8,128)(2,1)}, bf16[64,2048]{1,0:T(8,128)(2,1)}, u32[]{:S(2)}, u32[]{:S(2)}) collective-permute-start(bf16[64,2048]{1,0:T(8,128)(2,1)} %copy.218), channel_id=1, source_target_pairs={{1,0},{2,1},{3,2},{4,3},{5,4},{6,5},{7,6},{8,7},{9,8},{10,9},{11,1... | collective-permute-start | bytes 786440 | tf_op jit(solution)/shard_map/ppermute | solution.py:23
  58.3 8.1 copy-start.14
  60.5 80.1 %copy-start.6 = (bf16[2,64,16,64]{3,2,1,0:T(8,128)(2,1)}, bf16[2,64,16,64]{3,2,1,0:T(8,128)(2,1)S(1)}, u32[]{:S(2)}) copy-start(bf16[2,64,16,64]{3,2,1,0:T(8,128)(2,1)S(1)} %reshape.398) | copy-start | bytes 786436
  63.9 11.2 %copy-start.9 = (bf16[128,1024]{0,1:T(8,128)(2,1)S(1)}, bf16[128,1024]{0,1:T(8,128)(2,1)}, u32[]{:S(2)}) copy-start(bf16[128,1024]{0,1:T(8,128)(2,1)} %copy.209) | copy-start | bytes 786436
  67.2 8.8 copy-start.11
  72.4 933.8 %all-reduce.4.cloned.1.call-start = ((), (), s32[]{:S(2)}) async-start(), calls=%async_computation.1 | async-start | bytes 1048576 | tf_op jit(solution)/shard_map/psum | solution.py:189
  77.2 3.1 copy-start.13
  139.1 1.0 copy-start.12
  140.6 2.5 copy-start.7
  305.1 1.3 copy-start.10
  306.9 344.6 %copy-start.4 = (f32[16,128,128]{1,2,0:T(8,128)}, f32[16,128,128]{1,2,0:T(8,128)S(1)}, u32[]{:S(2)}) copy-start(f32[16,128,128]{1,2,0:T(8,128)S(1)} %get-tuple-element.59) | copy-start | bytes 3145732
  651.6 1.8 copy-start.5
  1029.6 4.4 copy-start.1
  1029.6 4.4 copy-start.2
  1036.7 1.7 copy-start.3
  1045.8 3.3 copy-start.15
  1053.7 1.9 copy-start.17
Sparse Core Ops, SparseCore 0:
  72.6 228.0 all-reduce.5
  649.5 219.8 all-reduce.3
where the time goes:
time: 1070 us; the launch traced here: 1060 us
  blocking collectives  692 us (65%)
  waiting for transfers between devices  207 us (19%)
  local copies, waits for them, and re-layouts  75.9 us (7%)
  other arithmetic  26.4 us (2%)
  starting transfers between devices  21.9 us (2%)
  matrix products  21.1 us (2%)
  between operations  18.9 us (2%)
    psum x1, blocking collectives, per_device(): lax.psum((jnp.sum(weights, axis=2), local_numer), 'ctx')  351 us
    pmax x1, blocking collectives, per_device(): peak_score = lax.pmax(local_peak, 'ctx')  341 us
    psum x1, waiting for transfers between devices, from_root(): return lax.psum(block, axis)  154 us
    ppermute x1, waiting for transfers between devices, padded_2(): lax.ppermute(lax.slice_in_dim(block, block.shape[dim] - width, None, axis...  50.7 us
  transfers between devices with their start and end apart: 5, of which 3 were waited for; matrix products, arithmetic and copies ran while one was open for 6% of the time, Pallas kernels for 0%

commit v1 on v0

v1 whole, which is shorter than its diff:
```python
import functools
import math

import jax
import jax.numpy as jnp
from jax import lax
from jax.experimental import pallas as pl
from jax.experimental.pallas import tpu as pltpu
from jax.sharding import PartitionSpec as P

BLOCK = 64
G = 2
NX, NY, NZ = 4, 4, 8
BATCHES = (10, 10, 10, 20, 12, 10, 14)
MESH = pl.DeviceIdType.MESH
bf16 = jnp.bfloat16
f32 = jnp.float32


def swap_halves(x):
    return jnp.concatenate([x[:, 64:], x[:, :64]], axis=1)


def low_half(shape):
    return lax.broadcasted_iota(jnp.int32, shape, 1) < 64


def prep_kernel(heads, rand, queries, keys, values, rb, gb, payload, kvt, qt, candq, candkv, rtab,
                tab_v, tab_s, rb_s, seen, sem):
    count = NX * NY * NZ
    me = lax.axis_index("ctx")
    pairs = heads // 2
    copy_rb = pltpu.make_async_copy(rb, rb_s, sem.at[0])
    copy_rb.start()
    lanes = 2 * count
    first = jnp.full((1, lanes), 1e9, f32)
    last = jnp.full((1, lanes), -1.0, f32)
    lane = lax.broadcasted_iota(jnp.int32, (heads, lanes), 1)
    head = lax.broadcasted_iota(jnp.int32, (heads, lanes), 0)
    for r in range(rand):
        req = rb[r]
        mine = (req // 2) == me
        key = (((lane % 2) * heads + head) * rand + r) * 2 + req % 2
        key = key.astype(f32)
        first = jnp.minimum(first, jnp.min(jnp.where(mine, key, 1e9), axis=0, keepdims=True))
        last = jnp.maximum(last, jnp.max(jnp.where(mine, key, -1.0), axis=0, keepdims=True))
    first = jnp.minimum(first, pltpu.roll(first, lanes - 1, 1))
    last = jnp.maximum(last, pltpu.roll(last, lanes - 1, 1))

    def to_tile(key):
        key = jnp.clip(key, 0.0, float(4 * heads * rand - 1)).astype(jnp.int32)
        return (key % 2) * heads + (key // 2 // rand) % heads

    tab_v[0:1, :] = to_tile(first)
    tab_v[1:2, :] = to_tile(last)
    copy_tab = pltpu.make_async_copy(tab_v, tab_s, sem.at[1])
    copy_tab.start()
    low = low_half((BLOCK, 128))
    zero = jnp.zeros((BLOCK, 128), bf16)
    for b in range(2):
        rows = slice(b * BLOCK, (b + 1) * BLOCK)
        for p in range(pairs):
            cols = slice(p * 128, (p + 1) * 128)
            kr = swap_halves(keys[rows, cols])
            vn = values[rows, cols]
            qr = swap_halves(queries[rows, cols])
            kvt[b * heads + 2 * p] = jnp.where(low, vn, kr)
            kvt[b * heads + 2 * p + 1] = jnp.where(low, kr, vn)
            qt[2 * p, rows, :] = jnp.where(low, zero, qr)
            qt[2 * p + 1, rows, :] = jnp.where(low, qr, zero)
    for g in range(G):
        local = gb[g] % 2

        def pick(h, c):
            candkv[h, g] = kvt[local * heads + h]
            return c

        lax.fori_loop(0, heads, pick, 0)
        for p in range(pairs):
            candq[g * pairs + p] = queries[pl.ds(pl.multiple_of(local * BLOCK, BLOCK), BLOCK), p * 128:(p + 1) * 128]

    def clear(i, c):
        seen[i] = 0
        return c

    lax.fori_loop(0, count, clear, 0)
    copy_rb.wait()

    def mark(i, c):
        b = i // (heads * rand)
        h = (i // rand) % heads
        owner = rb_s[i % rand, h, 2 * me + b] // 2
        slot = seen[owner]
        rtab[i] = owner * 2 + slot
        seen[owner] = 1
        return c

    lax.fori_loop(0, 2 * heads * rand, mark, 0)
    copy_tab.wait()

    def fill(d, c):
        payload[2 * d] = kvt[tab_s[0, 2 * d]]
        payload[2 * d + 1] = kvt[tab_s[1, 2 * d]]
        return c

    lax.fori_loop(0, count, fill, 0)


def main_kernel(heads, rand, payload, kvt, qt, candq, candkv, hidden, weight, gain, gb, rtab, out,
                recv, win, recvq, zq, gq, recvkv, zkv, gkv, part, rpart, zpart, ghead, gctx, att,
                a2a_s, a2a_r, send, got, loc):
    count, plane = NX * NY * NZ, NX * NY
    pairs = heads // 2
    zrows = 2 * BLOCK // NZ
    me = lax.axis_index("ctx")
    x, z, y = me % NX, (me // NX) % NZ, me // (NX * NZ)
    pos = y * NX + x

    def at(px, pz, py):
        return {"ctx": (py * NZ + pz) * NX + px}

    def shifted(k):
        kx, kz, ky = k % NX, (k // NX) % NZ, k // (NX * NZ)
        return ((y + ky) % NY * NZ + (z + kz) % NZ) * NX + (x + kx) % NX

    def remote(src, dst, s, r, device):
        return pltpu.make_async_remote_copy(
            src_ref=src, dst_ref=dst, send_sem=s, recv_sem=r, device_id=device, device_id_type=MESH)

    barrier = pltpu.get_barrier_semaphore()

    def greet(k, c):
        pl.semaphore_signal(barrier, inc=1, device_id={"ctx": shifted(k)}, device_id_type=MESH)
        return c

    lax.fori_loop(1, count, greet, 0)
    pl.semaphore_wait(barrier, count - 1)

    issued = [1]

    def batch(n):
        lo = issued[0]
        hi = min(count, lo + n)
        issued[0] = hi

        def one(k, c):
            d = shifted((k * 37) % count)
            remote(payload.at[pl.ds(2 * d, 2)], recv.at[pl.ds(2 * me, 2)], a2a_s, a2a_r, {"ctx": d}).start()
            return c

        if hi > lo:
            lax.fori_loop(lo, hi, one, 0)

    def to_plane(fn, i):
        def one(k, c):
            p = ((y + k // NX) % NY) * NX + (x + k % NX) % NX
            src, dst = fn(p)
            remote(src, dst, send.at[i], got.at[i], at(p % NX, z, p // NX)).start()
            return c

        lax.fori_loop(1, plane, one, 0)

    def to_line(fn, i):
        def one(k, c):
            pz = (z + k) % NZ
            src, dst = fn(pz)
            remote(src, dst, send.at[i], got.at[i], at(x, pz, y)).start()
            return c

        lax.fori_loop(1, NZ, one, 0)

    def wait_got(ref, i):
        pltpu.make_async_copy(ref, ref, got.at[i]).wait()

    def wait_sent(ref, i):
        pltpu.make_async_copy(ref, ref, send.at[i]).wait()

    def owner_of(g):
        return gb[g] // 2

    def pos_of(d):
        return (d // (NX * NZ)) * NX + d % NX

    def z_of(d):
        return (d // NX) % NZ

    own = [
        pltpu.make_async_copy(candq.at[pos], recvq.at[pos], loc.at[0]),
        pltpu.make_async_copy(candkv.at[pos], recvkv.at[pos], loc.at[1]),
        pltpu.make_async_copy(payload.at[pl.ds(2 * me, 2)], recv.at[pl.ds(2 * me, 2)], loc.at[2]),
    ]
    for c in own:
        c.start()

    to_plane(lambda p: (candq.at[p], recvq.at[pos]), 0)
    to_plane(lambda p: (candkv.at[p], recvkv.at[pos]), 1)
    batch(BATCHES[0])
    own[0].wait()
    wait_got(recvq.at[pl.ds(0, plane - 1)], 0)
    my_g = pos // pairs
    q_owner = owner_of(my_g)
    zq[z] = recvq[pos_of(q_owner)]
    batch(2)
    to_line(lambda p: (zq.at[z], zq.at[z]), 2)
    batch(BATCHES[1] - 2)
    own[1].wait()
    wait_got(recvkv.at[pl.ds(0, plane - 1)], 1)
    for g in range(G):
        zkv[z, g] = recvkv[pos_of(owner_of(g)), g]
    wait_got(zq.at[pl.ds(0, NZ - 1)], 2)
    gq[pos] = zq[z_of(q_owner)]
    batch(2)
    to_plane(lambda p: (gq.at[pos], gq.at[pos]), 3)
    to_line(lambda p: (zkv.at[z], zkv.at[z]), 4)
    nxt, prv = (me + 1) % count, (me + count - 1) % count
    w0 = remote(kvt.at[pl.ds(heads, heads)], win.at[0], send.at[5], got.at[5], {"ctx": nxt})
    w1 = remote(kvt.at[pl.ds(0, heads)], win.at[1], send.at[6], got.at[6], {"ctx": prv})
    batch(BATCHES[2] - 2)
    wait_got(gq.at[pl.ds(0, plane - 1)], 3)

    lane = lax.broadcasted_iota(jnp.int32, (2 * BLOCK, 128), 1)
    low = lane < 64

    def score(q, tiles):
        return lax.dot_general(q, tiles, (((1,), (1,)), ((), ())), preferred_element_type=f32) * 0.125

    def send_part(h):
        @pl.when(h != pos)
        def _():
            remote(part.at[h], rpart.at[pos], send.at[7], got.at[7], at(h % NX, z, h // NX)).start()

    per_pair = max(1, BATCHES[3] // pairs)

    def partial(i, c):
        @pl.when(i > 0)
        def _():
            before = (pos // 2 + i) % pairs
            send_part(2 * before)
            send_part(2 * before + 1)

        p = (pos // 2 + i + 1) % pairs
        q = jnp.concatenate([gq[p], gq[pairs + p]], axis=0)
        q = swap_halves(q)
        for odd in range(2):
            h = 2 * p + odd
            tiles = jnp.concatenate([kvt[h], kvt[heads + h]], axis=0)
            mine = low if odd else jnp.logical_not(low)
            s = score(jnp.where(mine, q, jnp.zeros_like(q)), tiles)
            top = jnp.max(s, axis=1, keepdims=True)
            e = jnp.exp(s - top)
            total = jnp.sum(e, axis=1, keepdims=True)
            hi = e.astype(bf16)
            lo = (e - hi.astype(f32)).astype(bf16)
            numer = jnp.dot(hi, tiles, preferred_element_type=f32) + jnp.dot(lo, tiles, preferred_element_type=f32)
            stats = jnp.where(lane % 64 < 32, total, top)
            part[h] = jnp.where(mine, stats, numer)
        return c

    lax.fori_loop(0, pairs, partial, 0)
    batch(2)
    last_pair = pos // 2
    send_part(2 * last_pair)
    send_part(2 * last_pair + 1)
    own_part = pltpu.make_async_copy(part.at[pos], rpart.at[pos], loc.at[3])
    own_part.start()
    batch(BATCHES[3])
    w0.start()
    w1.start()
    wait_got(zkv.at[pl.ds(0, NZ - 1)], 4)
    for g in range(G):
        gkv[pos, g] = zkv[z_of(owner_of(g)), g]
    batch(2)
    to_plane(lambda p: (gkv.at[pos], gkv.at[pos]), 8)

    odd_head = pos % 2 == 1

    def merge(ref, n, rows):
        ln = lax.broadcasted_iota(jnp.int32, (rows, 128), 1)
        stat = (ln < 64) == odd_head
        is_top = jnp.logical_and(stat, ln % 64 >= 32)
        tops = [jnp.max(jnp.where(is_top, ref[j], -3e38), axis=1, keepdims=True) for j in range(n)]
        top = functools.reduce(jnp.maximum, tops)
        acc = functools.reduce(jnp.add, [ref[j] * jnp.exp(tops[j] - top) for j in range(n)])
        is_total = jnp.logical_and(stat, ln % 64 < 32)
        total = jnp.max(jnp.where(is_total, acc, 0.0), axis=1, keepdims=True)
        return jnp.where(is_top, top, acc), total

    own_part.wait()
    wait_got(rpart.at[pl.ds(0, plane - 1)], 7)

    def merge_rows(i, c):
        rows = pl.ds(pl.multiple_of(i * zrows, zrows), zrows)
        merged, _ = merge(rpart.at[:, rows, :], plane, zrows)
        zsum_ref = part.at[0]
        zsum_ref[rows, :] = merged
        return c

    wait_sent(part.at[pl.ds(0, plane - 1)], 7)
    lax.fori_loop(0, NZ, merge_rows, 0)
    own_z = pltpu.make_async_copy(
        part.at[0, pl.ds(pl.multiple_of(z * zrows, zrows), zrows)], zpart.at[z], loc.at[4])
    batch(2)
    to_line(lambda p: (part.at[0, pl.ds(pl.multiple_of(p * zrows, zrows), zrows)], zpart.at[z]), 9)
    own_z.start()
    batch(BATCHES[4] - 2)
    own_z.wait()
    wait_got(zpart.at[pl.ds(0, NZ - 1)], 9)
    acc, total = merge(zpart, NZ, zrows)
    my_rows = pl.ds(pl.multiple_of(z * zrows, zrows), zrows)
    ghead[z] = (acc / total).astype(bf16)
    batch(2)
    to_line(lambda p: (ghead.at[z], ghead.at[z]), 10)
    batch(BATCHES[5] - 2)
    wait_got(ghead.at[pl.ds(0, NZ - 1)], 10)
    own_g = pltpu.make_async_copy(ghead, gctx.at[pos], loc.at[5])
    own_g.start()
    to_plane(lambda p: (ghead, gctx.at[pos]), 11)
    batch(BATCHES[6])
    batch(count)
    own_g.wait()
    own[2].wait()
    wait_got(gctx.at[pl.ds(0, plane - 1)], 11)
    wait_got(gkv.at[pl.ds(0, plane - 1)], 8)
    w0.wait_recv()
    w1.wait_recv()
    pltpu.make_async_copy(recv.at[pl.ds(0, 2 * count - 2)], recv.at[pl.ds(0, 2 * count - 2)], a2a_r).wait()

    row = lax.broadcasted_iota(jnp.int32, (2 * BLOCK, 6 * BLOCK), 0)
    col = lax.broadcasted_iota(jnp.int32, (2 * BLOCK, 6 * BLOCK), 1)
    first_rows = row < BLOCK
    is_prev = col < BLOCK
    is_next = jnp.logical_and(col >= 3 * BLOCK, col < 4 * BLOCK)
    no_prev = jnp.logical_or(jnp.logical_not(first_rows), me == 0)
    no_next = jnp.logical_or(first_rows, me == count - 1)
    hidden_keys = jnp.logical_or(jnp.logical_and(is_prev, no_prev), jnp.logical_and(is_next, no_next))
    low_b = low_half((BLOCK, 128))

    def attend(p, c):
        results = []
        for odd in range(2):
            h = 2 * p + odd
            tiles = jnp.concatenate(
                [win[0, h], kvt[h], kvt[heads + h], win[1, h], gkv[h, 0], gkv[h, 1]], axis=0)
            q = qt[h]
            s = jnp.where(hidden_keys, -1e30, score(q, tiles))
            rand_tiles = []
            rand_scores = []
            for b in range(2):
                base = (b * heads + h) * rand
                t = jnp.concatenate([recv[rtab[base + r]] for r in range(rand)], axis=0)
                rand_tiles.append(t)
                rand_scores.append(score(q[b * BLOCK:(b + 1) * BLOCK], t))
            sr = jnp.concatenate(rand_scores, axis=0)
            top = jnp.maximum(jnp.max(s, axis=1, keepdims=True), jnp.max(sr, axis=1, keepdims=True))
            e = jnp.exp(s - top)
            er = jnp.exp(sr - top)
            inv = 1.0 / (jnp.sum(e, axis=1, keepdims=True) + jnp.sum(er, axis=1, keepdims=True))
            pr = (er * inv).astype(bf16)
            ctx = jnp.dot((e * inv).astype(bf16), tiles, preferred_element_type=f32)
            ctx = ctx + jnp.concatenate(
                [jnp.dot(pr[b * BLOCK:(b + 1) * BLOCK], rand_tiles[b], preferred_element_type=f32) for b in range(2)],
                axis=0)
            results.append(ctx)
        both = jnp.where(low, results[0], results[1])
        cols = pl.ds(pl.multiple_of(p * 128, 128), 128)
        for b in range(2):
            rows = both[b * BLOCK:(b + 1) * BLOCK].astype(bf16)
            for g in range(G):
                ge = gctx[2 * p].reshape(2 * BLOCK, 128)[g * BLOCK:(g + 1) * BLOCK]
                go = gctx[2 * p + 1].reshape(2 * BLOCK, 128)[g * BLOCK:(g + 1) * BLOCK]
                rows = jnp.where(2 * me + b == gb[g], jnp.where(low_b, ge, go), rows)
            att[b * BLOCK:(b + 1) * BLOCK, cols] = rows
        return c

    lax.fori_loop(0, pairs, attend, 0)
    mixed = hidden[...].astype(f32) + jnp.dot(att[...], weight[...], preferred_element_type=f32)
    mean = jnp.mean(mixed, axis=1, keepdims=True)
    centred = mixed - mean
    var = jnp.mean(centred * centred, axis=1, keepdims=True)
    out[...] = (centred * lax.rsqrt(var + 1e-05) * gain[...]).astype(bf16)

    wait_sent(candq.at[pl.ds(0, plane - 1)], 0)
    wait_sent(candkv.at[pl.ds(0, plane - 1)], 1)
    wait_sent(zq.at[pl.ds(0, NZ - 1)], 2)
    wait_sent(gq.at[pl.ds(0, plane - 1)], 3)
    wait_sent(zkv.at[pl.ds(0, NZ - 1)], 4)
    w0.wait_send()
    w1.wait_send()
    wait_sent(gkv.at[pl.ds(0, plane - 1)], 8)
    wait_sent(zpart.at[pl.ds(0, NZ - 1)], 9)
    wait_sent(ghead.at[pl.ds(0, NZ - 1)], 10)
    wait_sent(gctx.at[pl.ds(0, plane - 1)], 11)
    pltpu.make_async_copy(recv.at[pl.ds(0, 2 * count - 2)], recv.at[pl.ds(0, 2 * count - 2)], a2a_s).wait()


def per_device(queries, keys, values, hidden, out_weight, norm_gain, random_blocks, global_blocks):
    row_count, width = queries.shape
    heads, rand = random_blocks.shape[1:]
    count, plane = NX * NY * NZ, NX * NY
    zrows = 2 * BLOCK // NZ
    vmem = pl.BlockSpec(memory_space=pltpu.VMEM)
    smem = pl.BlockSpec(memory_space=pltpu.SMEM)
    anym = pl.BlockSpec(memory_space=pl.ANY)
    shape = jax.ShapeDtypeStruct
    payload, kvt, qt, candq, candkv, rtab = pl.pallas_call(
        functools.partial(prep_kernel, heads, rand),
        out_shape=(
            shape((2 * count, BLOCK, 128), bf16),
            shape((2 * heads, BLOCK, 128), bf16),
            shape((heads, 2 * BLOCK, 128), bf16),
            shape((plane, BLOCK, 128), bf16),
            shape((heads, G, BLOCK, 128), bf16),
            shape((2 * heads * rand,), jnp.int32),
        ),
        in_specs=[vmem, vmem, vmem, vmem, smem],
        out_specs=(vmem, vmem, vmem, vmem, vmem, smem),
        scratch_shapes=[
            pltpu.VMEM((2, 2 * count), jnp.int32),
            pltpu.SMEM((2, 2 * count), jnp.int32),
            pltpu.SMEM((rand, heads, 2 * count), jnp.int32),
            pltpu.SMEM((count,), jnp.int32),
            pltpu.SemaphoreType.DMA((2,)),
        ],
        compiler_params=pltpu.CompilerParams(vmem_limit_bytes=24 << 20),
        name="prep",
    )(queries, keys, values, jnp.transpose(random_blocks, (2, 1, 0)), global_blocks)
    return pl.pallas_call(
        functools.partial(main_kernel, heads, rand),
        out_shape=shape((row_count, width), bf16),
        in_specs=[anym, vmem, vmem, vmem, vmem, vmem, vmem, vmem, smem, smem],
        out_specs=vmem,
        scratch_shapes=[
            pltpu.VMEM((2 * count, BLOCK, 128), bf16),
            pltpu.VMEM((2, heads, BLOCK, 128), bf16),
            pltpu.VMEM((plane, BLOCK, 128), bf16),
            pltpu.VMEM((NZ, BLOCK, 128), bf16),
            pltpu.VMEM((plane, BLOCK, 128), bf16),
            pltpu.VMEM((plane, G, BLOCK, 128), bf16),
            pltpu.VMEM((NZ, G, BLOCK, 128), bf16),
            pltpu.VMEM((plane, G, BLOCK, 128), bf16),
            pltpu.VMEM((heads, 2 * BLOCK, 128), f32),
            pltpu.VMEM((heads, 2 * BLOCK, 128), f32),
            pltpu.VMEM((NZ, zrows, 128), f32),
            pltpu.VMEM((NZ, zrows, 128), bf16),
            pltpu.VMEM((heads, NZ, zrows, 128), bf16),
            pltpu.VMEM((row_count, width), bf16),
            pltpu.SemaphoreType.DMA,
            pltpu.SemaphoreType.DMA,
            pltpu.SemaphoreType.DMA((12,)),
            pltpu.SemaphoreType.DMA((12,)),
            pltpu.SemaphoreType.DMA((6,)),
        ],
        compiler_params=pltpu.CompilerParams(
            collective_id=0, has_side_effects=True, vmem_limit_bytes=40 << 20),
        name="main",
    )(payload, kvt, qt, candq, candkv, hidden, out_weight, norm_gain.reshape(1, width), global_blocks, rtab)


def solution(mesh):
    placed = (
        P(("dp", "ctx"), None),
        P(("dp", "ctx"), None),
        P(("dp", "ctx"), None),
        P(("dp", "ctx"), None),
        P(),
        P(),
        P("dp", None, None),
        P("dp"),
    )
    return jax.shard_map(
        per_device, mesh=mesh, in_specs=placed, out_specs=P(("dp", "ctx"), None), check_vma=False
    )
```

time: 1070 us -> 153 us (0.14)
  blocking collectives: 692 us -> 0 us
  waiting for transfers between devices: 207 us -> 0 us
  Pallas kernels: 0 us -> 144 us
  local copies, waits for them, and re-layouts: 75.9 us -> 8.88 us
  other arithmetic: 26.4 us -> 0 us
  starting transfers between devices: 21.9 us -> 0 us
  matrix products: 21.1 us -> 0 us
  between operations: 18.9 us -> 0.03 us
    psum x1 -> x0, blocking collectives: 351 us -> none  [per_device(): lax.psum((jnp.sum(weights, axis=2), local_numer), 'ctx')]
    pmax x1 -> x0, blocking collectives: 341 us -> none  [per_device(): peak_score = lax.pmax(local_peak, 'ctx')]
    psum x2 -> x0, waiting for transfers between devices: 154 us -> none  [the longest x1 154 us: from_root(): return lax.psum(block, axis)]
    pallas_call x0 -> x2, Pallas kernels: none -> 144 us  [the longest x1 137 us: per_device(): pl.pallas_call(functools.partial(main_kernel, heads, rand), out_shape=sha...]
    ppermute x2 -> x0, waiting for transfers between devices: 52.8 us -> none  [the longest x1 50.7 us: padded_2(): lax.ppermute(lax.slice_in_dim(block, block.shape[dim] - width, None, axis...]
    dot_general x8 -> x0, matrix products: 19.3 us -> none  [the longest x1 3.8 us: group_context(): jnp.einsum('bqhd,bhrkd->bhqrk', query_blocks, tile_rows[..., :head_size],...]
    reshape x11 -> x0, local copies, waits for them, and re-layouts: 16.6 us -> none  [the longest x1 3.65 us: group_context(): s_window.reshape(group_size, head_count, BLOCK, window_span * BLOCK)]
    slice x11 -> x0, local copies, waits for them, and re-layouts: 16.2 us -> none  [the longest x2 4.2 us: group_context(): probabilities[..., :window_span * BLOCK]]
  transfers between devices with their start and end apart: 5 -> 0, of which waited for: 3 -> 0; matrix products, arithmetic and copies ran while one was open for 6% -> 0% of each run, Pallas kernels for 0% -> 0%
where the time goes in v1:
time: 153 us; the launch traced here: 152 us
  Pallas kernels  144 us (94%)
  local copies, waits for them, and re-layouts  8.88 us (6%)
    pallas_call x1, Pallas kernels, per_device(): pl.pallas_call(functools.partial(main_kernel, heads, rand), out_shape=sha...  137 us
    unnamed x19, local copies, waits for them, and re-layouts  8.88 us
    pallas_call x1, Pallas kernels, per_device(): pl.pallas_call(functools.partial(prep_kernel, heads, rand), out_shape=(sh...  6.68 us

profile of v1, /device:TPU:6, one launch (start us, length us, event | category | flops | bytes accessed | tf_op | source)
XLA Modules:
  0.0 152.5 jit_solution(5386506561728721398)
XLA Ops:
  0.0 0.0 copy-start.1
  0.0 0.9 copy-done.1
  1.0 0.0 copy-start.2
  1.0 0.9 copy-done.2
  1.9 0.0 copy-start.3
  1.9 0.9 copy-done.3
  2.9 0.0 copy-start.5
  2.9 0.8 copy-done.5
  3.7 0.0 copy-start.7
  3.7 0.7 copy-done.7
  4.3 6.7 %prep.1 = (bf16[256,64,128]{2,1,0:T(8,128)(2,1)S(1)}, bf16[32,64,128]{2,1,0:T(8,128)(2,1)S(1)}, bf16[16,128,128]{2,1,0:T(8,128)(2,1)S(1)}, bf16[16,64,128]{2,1,0...) custom-call(bf16[128,1024]{1,0:T(8,128)(2,1)S(1)} %copy-done.1, bf16[128,1024]{1,0:T(8,128)(2,1)S(1)} %copy-done.2, ...), custom_call_target="tpu_custom_call" | custom-call | tf_op jit(solution)/shard_map/prep/pallas_call | solution.py:405
  11.0 0.0 copy-start
  11.0 1.6 %copy-done = bf16[1024,1024]{1,0:T(8,128)(2,1)S(1)} copy-done((bf16[1024,1024]{1,0:T(8,128)(2,1)S(1)}, bf16[1024,1024]{1,0:T(8,128)(2,1)}, u32[]{:S(2)}) %copy-start) | copy-done | bytes 2097176
  12.6 0.0 copy-start.4
  12.6 0.9 copy-done.4
  13.5 0.0 copy-start.6
  13.5 0.7 copy-done.6
  14.2 0.0 copy-start.8
  14.2 0.7 copy-done.8
  14.9 136.9 %main.1 = bf16[128,1024]{1,0:T(8,128)(2,1)S(1)} custom-call(bf16[256,64,128]{2,1,0:T(8,128)(2,1)S(1)} %get-tuple-element.11.payload, bf16[32,64,128]{2,1,0:T(8,128)(2,1)S(1)} %get-tuple-element.12.kvt, bf16[16,128,128]{2,1,0:T(8,128)(2,1)S(1)} %get-tuple-element.13.qt, bf16[16,64,128]{2,1,0:T(8,128)(2,1)S(1)} %get-tuple-element.14.candq, ...), custom_call_target="tpu_custom_call" | custom-call | tf_op jit(solution)/shard_map/main/pallas_call | solution.py:427
  151.8 0.7 copy.10
Async XLA Ops:
  0.0 0.9 copy-start.1
  1.0 0.9 copy-start.2
  1.9 0.9 copy-start.3
  2.9 0.8 copy-start.5
  3.7 0.7 copy-start.7
  11.0 1.6 %copy-start = (bf16[1024,1024]{1,0:T(8,128)(2,1)S(1)}, bf16[1024,1024]{1,0:T(8,128)(2,1)}, u32[]{:S(2)}) copy-start(bf16[1024,1024]{1,0:T(8,128)(2,1)} %weight.1) | copy-start | bytes 6291460
  12.6 0.9 copy-start.4
  13.5 0.7 copy-start.6
  14.2 0.7 copy-start.8

commit v2 on v1

v2 whole, which is shorter than its diff:
```python
import functools

import jax
import jax.numpy as jnp
from jax import lax
from jax.experimental import pallas as pl
from jax.experimental.pallas import tpu as pltpu
from jax.sharding import PartitionSpec as P

BLOCK = 64
G = 2
NX, NY, NZ = 4, 4, 8
BATCHES = (10, 10, 10, 20, 12, 10, 14)
MESH = pl.DeviceIdType.MESH
bf16 = jnp.bfloat16
f32 = jnp.float32


def swap_halves(x):
    return jnp.concatenate([x[:, 64:], x[:, :64]], axis=1)


def low_half(shape):
    return lax.broadcasted_iota(jnp.int32, shape, 1) < 64


def table_kernel(heads, rand, rb, tab, rtab, tab_v, rtab_v, sem):
    count = NX * NY * NZ
    me = lax.axis_index("ctx")
    lanes = 2 * count
    first = jnp.full((1, lanes), 1e9, f32)
    last = jnp.full((1, lanes), -1.0, f32)
    lane_d = lax.broadcasted_iota(jnp.int32, (heads, lanes), 1)
    head_d = lax.broadcasted_iota(jnp.int32, (heads, lanes), 0)
    for r in range(rand):
        req = rb[r]
        mine = (req // 2) == me
        key = (((lane_d % 2) * heads + head_d) * rand + r) * 2 + req % 2
        key = key.astype(f32)
        first = jnp.minimum(first, jnp.min(jnp.where(mine, key, 1e9), axis=0, keepdims=True))
        last = jnp.maximum(last, jnp.max(jnp.where(mine, key, -1.0), axis=0, keepdims=True))
    first = jnp.minimum(first, pltpu.roll(first, lanes - 1, 1))
    last = jnp.maximum(last, pltpu.roll(last, lanes - 1, 1))

    def to_tile(key):
        key = jnp.clip(key, 0.0, float(4 * heads * rand - 1)).astype(jnp.int32)
        return (key % 2) * heads + (key // 2 // rand) % heads

    tab_v[0:1, :] = to_tile(first)
    tab_v[1:2, :] = to_tile(last)
    copy_tab = pltpu.make_async_copy(tab_v, tab, sem.at[0])
    copy_tab.start()

    pick_c = (lax.broadcasted_iota(jnp.int32, (lanes, 128), 0) == 2 * me + lax.broadcasted_iota(
        jnp.int32, (lanes, 128), 1)).astype(f32).astype(bf16)
    pick_r = (lax.broadcasted_iota(jnp.int32, (8, lanes), 1) == 2 * me + lax.broadcasted_iota(
        jnp.int32, (8, lanes), 0)).astype(f32).astype(bf16)
    pad = jnp.zeros((128 - heads, lanes), bf16)
    own_c, own_r = [], []
    for r in range(rand):
        ids = rb[r].astype(f32).astype(bf16)
        as_col = jnp.dot(ids, pick_c, preferred_element_type=f32).astype(jnp.int32) // 2
        as_row = lax.dot_general(pick_r, jnp.concatenate([ids, pad], axis=0), (((1,), (1,)), ((), ())),
                                 preferred_element_type=f32).astype(jnp.int32) // 2
        own_c.append([as_col[:, b:b + 1] for b in range(2)])
        own_r.append([as_row[b:b + 1, :] for b in range(2)])
    hc = lax.broadcasted_iota(jnp.int32, (heads, 128), 0)
    hr = lax.broadcasted_iota(jnp.int32, (heads, 128), 1)
    table = jnp.zeros((heads, 128), jnp.int32)
    for b in range(2):
        for r in range(rand):
            again = jnp.zeros((heads, 128), f32)
            for b2 in range(b + 1):
                for r2 in range(rand):
                    if b2 < b:
                        before = hr < heads
                    elif r2 < r:
                        before = hr <= hc
                    else:
                        before = hr < hc
                    same = jnp.logical_and(own_c[r][b] == own_r[r2][b2], before)
                    again = jnp.maximum(again, jnp.where(same, 1.0, 0.0))
            slot = jnp.max(again, axis=1, keepdims=True).astype(jnp.int32)
            table = jnp.where(hr == b * rand + r, own_c[r][b] * 2 + slot, table)
    rtab_v[...] = table
    copy_rtab = pltpu.make_async_copy(rtab_v, rtab, sem.at[1])
    copy_rtab.start()
    copy_tab.wait()
    copy_rtab.wait()


def main_kernel(heads, rand, queries_h, keys_h, values_h, hidden_h, weight_h, gain_h, gb, tab_s, rtab_s, out,
                queries, keys, values, hidden, weight, gain, payload, kvt, qt, qpair, candq, candkv,
                recv, win, recvq, zq, gq, recvkv, selkv, zrkv, zkv, gkv, part, rpart, zsum, zpart, ghead, gctx,
                att, early, stats, a2a_s, a2a_r, send, got, loc, load):
    count, plane = NX * NY * NZ, NX * NY
    pairs = heads // 2
    half = NZ // G
    zrows = 2 * BLOCK // NZ
    me = lax.axis_index("ctx")
    x, z, y = me % NX, (me // NX) % NZ, me // (NX * NZ)
    pos = y * NX + x

    def at(px, pz, py):
        return {"ctx": (py * NZ + pz) * NX + px}

    def shifted(k):
        kx, kz, ky = k % NX, (k // NX) % NZ, k // (NX * NZ)
        return ((y + ky) % NY * NZ + (z + kz) % NZ) * NX + (x + kx) % NX

    def remote(src, dst, s, r, device):
        return pltpu.make_async_remote_copy(
            src_ref=src, dst_ref=dst, send_sem=s, recv_sem=r, device_id=device, device_id_type=MESH)

    loads = [
        pltpu.make_async_copy(src, dst, load.at[i])
        for i, (src, dst) in enumerate((
            (queries_h, queries), (keys_h, keys), (values_h, values),
            (hidden_h, hidden), (weight_h, weight), (gain_h, gain)))
    ]
    for c in loads:
        c.start()

    barrier = pltpu.get_barrier_semaphore()

    def greet(k, c):
        pl.semaphore_signal(barrier, inc=1, device_id={"ctx": shifted(k)}, device_id_type=MESH)
        return c

    lax.fori_loop(1, count, greet, 0)

    for c in loads[:3]:
        c.wait()
    low_b = low_half((BLOCK, 128))
    for b in range(2):
        for p in range(pairs):
            qpair[b * pairs + p] = queries[b * BLOCK:(b + 1) * BLOCK, p * 128:(p + 1) * 128]
    for g in range(G):
        for p in range(pairs):
            candq[g * pairs + p] = qpair[gb[g] % 2 * pairs + p]
    for b in range(2):
        rows = slice(b * BLOCK, (b + 1) * BLOCK)
        for p in range(pairs):
            cols = slice(p * 128, (p + 1) * 128)
            kr = swap_halves(keys[rows, cols])
            vn = values[rows, cols]
            kvt[b * heads + 2 * p] = jnp.where(low_b, vn, kr)
            kvt[b * heads + 2 * p + 1] = jnp.where(low_b, kr, vn)

    def pick(h, c):
        for g in range(G):
            candkv[h, half * g:half * (g + 1)] = kvt[gb[g] % 2 * heads + h].reshape(half, BLOCK // half, 128)
        return c

    lax.fori_loop(0, heads, pick, 0)

    def fill(i, c):
        for u in range(4):
            d = 4 * i + u
            payload[2 * d] = kvt[tab_s[0, 2 * d]]
            payload[2 * d + 1] = kvt[tab_s[1, 2 * d]]
        return c

    lax.fori_loop(0, count // 4, fill, 0)
    zero_b = jnp.zeros((BLOCK, 128), bf16)
    for b in range(2):
        rows = slice(b * BLOCK, (b + 1) * BLOCK)
        for p in range(pairs):
            qr = swap_halves(queries[rows, p * 128:(p + 1) * 128])
            qt[2 * p, rows, :] = jnp.where(low_b, zero_b, qr)
            qt[2 * p + 1, rows, :] = jnp.where(low_b, qr, zero_b)
    pl.semaphore_wait(barrier, count - 1)

    issued = [1]

    def batch(n):
        lo = issued[0]
        hi = min(count, lo + n)
        issued[0] = hi

        def one(k, c):
            d = shifted((k * 37) % count)
            remote(payload.at[pl.ds(2 * d, 2)], recv.at[pl.ds(2 * me, 2)], a2a_s, a2a_r, {"ctx": d}).start()
            return c

        if hi > lo:
            lax.fori_loop(lo, hi, one, 0)

    def to_plane(fn, i):
        def one(k, c):
            p = ((y + k // NX) % NY) * NX + (x + k % NX) % NX
            src, dst = fn(p)
            remote(src, dst, send.at[i], got.at[i], at(p % NX, z, p // NX)).start()
            return c

        lax.fori_loop(1, plane, one, 0)

    def to_line(fn, i):
        def one(k, c):
            pz = (z + k) % NZ
            src, dst = fn(pz)
            remote(src, dst, send.at[i], got.at[i], at(x, pz, y)).start()
            return c

        lax.fori_loop(1, NZ, one, 0)

    def wait_got(ref, i):
        pltpu.make_async_copy(ref, ref, got.at[i]).wait()

    def wait_sent(ref, i):
        pltpu.make_async_copy(ref, ref, send.at[i]).wait()

    def owner_of(g):
        return gb[g] // 2

    def pos_of(d):
        return (d // (NX * NZ)) * NX + d % NX

    def z_of(d):
        return (d // NX) % NZ

    own = [
        pltpu.make_async_copy(candq.at[pos], recvq.at[pos], loc.at[0]),
        pltpu.make_async_copy(candkv.at[pos], recvkv.at[pos], loc.at[1]),
        pltpu.make_async_copy(payload.at[pl.ds(2 * me, 2)], recv.at[pl.ds(2 * me, 2)], loc.at[2]),
    ]
    for c in own:
        c.start()

    to_plane(lambda p: (candq.at[p], recvq.at[pos]), 0)
    to_plane(lambda p: (candkv.at[p], recvkv.at[pos]), 1)
    batch(BATCHES[0])
    own[0].wait()
    wait_got(recvq.at[pl.ds(0, plane - 1)], 0)
    my_g = pos // pairs
    q_owner = owner_of(my_g)
    zq[z] = recvq[pos_of(q_owner)]
    batch(2)
    to_line(lambda p: (zq.at[z], zq.at[z]), 2)
    batch(BATCHES[1] - 2)
    wait_got(zq.at[pl.ds(0, NZ - 1)], 2)
    gq[pos] = zq[z_of(q_owner)]
    batch(2)
    to_plane(lambda p: (gq.at[pos], gq.at[pos]), 3)
    batch(BATCHES[2] - 2)
    own[1].wait()
    wait_got(recvkv.at[pl.ds(0, plane - 1)], 1)

    for g in range(G):
        selkv[g * half:(g + 1) * half] = recvkv[pos_of(owner_of(g))][g * half:(g + 1) * half]
    own_kv = pltpu.make_async_copy(selkv.at[z], zrkv.at[z], loc.at[8])
    batch(2)
    to_line(lambda p: (selkv.at[p], zrkv.at[z]), 4)
    own_kv.start()
    nxt, prv = (me + 1) % count, (me + count - 1) % count
    w0 = remote(kvt.at[pl.ds(heads, heads)], win.at[0], send.at[5], got.at[5], {"ctx": nxt})
    w1 = remote(kvt.at[pl.ds(0, heads)], win.at[1], send.at[6], got.at[6], {"ctx": prv})
    wait_got(gq.at[pl.ds(0, plane - 1)], 3)

    lane = lax.broadcasted_iota(jnp.int32, (2 * BLOCK, 128), 1)
    low = lane < 64

    def score(q, tiles):
        return lax.dot_general(q, tiles, (((1,), (1,)), ((), ())), preferred_element_type=f32) * 0.125

    def send_part(h):
        @pl.when(h != pos)
        def _():
            remote(part.at[h], rpart.at[pos], send.at[7], got.at[7], at(h % NX, z, h // NX)).start()

    per_pair = max(1, BATCHES[3] // pairs)

    def partial(i, c):
        @pl.when(i > 0)
        def _():
            before = (pos // 2 + i) % pairs
            send_part(2 * before)
            send_part(2 * before + 1)

        p = (pos // 2 + i + 1) % pairs
        q = jnp.concatenate([gq[p], gq[pairs + p]], axis=0)
        q = swap_halves(q)
        for odd in range(2):
            h = 2 * p + odd
            tiles = jnp.concatenate([kvt[h], kvt[heads + h]], axis=0)
            mine = low if odd else jnp.logical_not(low)
            s = score(jnp.where(mine, q, jnp.zeros_like(q)), tiles)
            top = jnp.max(s, axis=1, keepdims=True)
            e = jnp.exp(s - top)
            total = jnp.sum(e, axis=1, keepdims=True)
            hi = e.astype(bf16)
            lo = (e - hi.astype(f32)).astype(bf16)
            numer = jnp.dot(hi, tiles, preferred_element_type=f32) + jnp.dot(lo, tiles, preferred_element_type=f32)
            part[h] = jnp.where(mine, jnp.where(lane % 64 < 32, total, top), numer)
        return c

    lax.fori_loop(0, pairs, partial, 0)
    batch(2)
    last_pair = pos // 2
    send_part(2 * last_pair)
    send_part(2 * last_pair + 1)
    own_part = pltpu.make_async_copy(part.at[pos], rpart.at[pos], loc.at[3])
    own_part.start()
    batch(BATCHES[3])
    w0.start()
    w1.start()
    own_kv.wait()
    wait_got(zrkv.at[pl.ds(0, NZ - 1)], 4)
    zkv[z] = zrkv[z_of(owner_of(z // half))]
    batch(2)
    to_line(lambda p: (zkv.at[z], zkv.at[z]), 12)

    odd_head = pos % 2 == 1

    def merge(ref, n, rows):
        ln = lax.broadcasted_iota(jnp.int32, (rows, 128), 1)
        side = (ln < 64) == odd_head
        is_top = jnp.logical_and(side, ln % 64 >= 32)
        terms = [ref[j] for j in range(n)]
        tops = [jnp.max(jnp.where(is_top, t, -3e38), axis=1, keepdims=True) for t in terms]
        top = functools.reduce(jnp.maximum, tops)
        acc = functools.reduce(jnp.add, [t * jnp.exp(tj - top) for t, tj in zip(terms, tops)])
        return acc, top, side, is_top, ln

    own_part.wait()
    wait_got(rpart.at[pl.ds(0, plane - 1)], 7)

    def merge_rows(i, c):
        rows = pl.ds(pl.multiple_of(i * zrows, zrows), zrows)
        acc, top, _, is_top, _ = merge(rpart.at[:, rows, :], plane, zrows)
        zsum[i] = jnp.where(is_top, top, acc)
        return c

    lax.fori_loop(0, NZ, merge_rows, 0)
    own_z = pltpu.make_async_copy(zsum.at[z], zpart.at[z], loc.at[4])
    batch(2)
    to_line(lambda p: (zsum.at[p], zpart.at[z]), 9)
    own_z.start()
    batch(BATCHES[4] - 2)
    wait_got(zkv.at[pl.ds(0, NZ - 1)], 12)
    own_gkv = pltpu.make_async_copy(zkv, gkv.at[pos], loc.at[9])
    own_gkv.start()
    to_plane(lambda p: (zkv, gkv.at[pos]), 8)
    own_z.wait()
    wait_got(zpart.at[pl.ds(0, NZ - 1)], 9)
    acc, _, side, _, ln = merge(zpart, NZ, zrows)
    total = jnp.max(jnp.where(jnp.logical_and(side, ln % 64 < 32), acc, -3e38), axis=1, keepdims=True)
    ghead[z] = (acc / total).astype(bf16)
    batch(2)
    to_line(lambda p: (ghead.at[z], ghead.at[z]), 10)
    batch(BATCHES[5] - 2)
    wait_got(ghead.at[pl.ds(0, NZ - 1)], 10)
    own_g = pltpu.make_async_copy(ghead, gctx.at[pos], loc.at[5])
    own_g.start()
    to_plane(lambda p: (ghead, gctx.at[pos]), 11)
    batch(count)
    own_gkv.wait()
    wait_got(gkv.at[pl.ds(0, plane - 1)], 8)
    w0.wait_recv()
    w1.wait_recv()

    row = lax.broadcasted_iota(jnp.int32, (2 * BLOCK, 6 * BLOCK), 0)
    col = lax.broadcasted_iota(jnp.int32, (2 * BLOCK, 6 * BLOCK), 1)
    first_rows = row < BLOCK
    is_prev = col < BLOCK
    is_next = jnp.logical_and(col >= 3 * BLOCK, col < 4 * BLOCK)
    no_prev = jnp.logical_or(jnp.logical_not(first_rows), me == 0)
    no_next = jnp.logical_or(first_rows, me == count - 1)
    hidden_keys = jnp.logical_or(jnp.logical_and(is_prev, no_prev), jnp.logical_and(is_next, no_next))
    def shared_tiles(h):
        return jnp.concatenate(
            [win[0, h], kvt[h], kvt[heads + h], win[1, h], gkv[h].reshape(2 * BLOCK, 128)], axis=0)

    def shared(p, c):
        for odd in range(2):
            h = 2 * p + odd
            s = jnp.where(hidden_keys, -1e30, score(qt[h], shared_tiles(h)))
            top = jnp.max(s, axis=1, keepdims=True)
            e = jnp.exp(s - top)
            early[h] = e
            stats[h, 0] = jnp.broadcast_to(top, (2 * BLOCK, 128))
            stats[h, 1] = jnp.broadcast_to(jnp.sum(e, axis=1, keepdims=True), (2 * BLOCK, 128))
        return c

    for p in range(pairs):
        shared(p, 0)
    own_g.wait()
    own[2].wait()
    for c in loads[3:]:
        c.wait()
    wait_got(gctx.at[pl.ds(0, plane - 1)], 11)
    pltpu.make_async_copy(recv.at[pl.ds(0, 2 * count - 2)], recv.at[pl.ds(0, 2 * count - 2)], a2a_r).wait()

    def attend(p, c):
        results = []
        for odd in range(2):
            h = 2 * p + odd
            q = qt[h]
            rand_tiles = []
            rand_scores = []
            for b in range(2):
                t = jnp.concatenate([recv[rtab_s[h, b * rand + r]] for r in range(rand)], axis=0)
                rand_tiles.append(t)
                rand_scores.append(score(q[b * BLOCK:(b + 1) * BLOCK], t))
            sr = jnp.concatenate(rand_scores, axis=0)
            cuts = [(c, min(c + 128, rand * BLOCK)) for c in range(0, rand * BLOCK, 128)]
            parts = [sr[:, lo:hi] for lo, hi in cuts]
            top_e = stats[h, 0]
            top = functools.reduce(jnp.maximum, [jnp.max(t, axis=1, keepdims=True) for t in parts] + [top_e])
            scale = jnp.exp(top_e - top)
            parts = [jnp.exp(t - top[:, :t.shape[1]]) for t in parts]
            inv = 1.0 / functools.reduce(
                jnp.add, [jnp.sum(t, axis=1, keepdims=True) for t in parts] + [stats[h, 1] * scale])
            pr = jnp.concatenate([(t * inv[:, :t.shape[1]]).astype(bf16) for t in parts], axis=1)
            ratio = scale * inv
            ps = jnp.concatenate([(early[h, :, c:c + 128] * ratio).astype(bf16) for c in range(0, 6 * BLOCK, 128)], axis=1)
            ctx = jnp.dot(ps, shared_tiles(h), preferred_element_type=f32)
            ctx = ctx + jnp.concatenate(
                [jnp.dot(pr[b * BLOCK:(b + 1) * BLOCK], rand_tiles[b], preferred_element_type=f32) for b in range(2)],
                axis=0)
            results.append(ctx)
        both = jnp.where(low, results[0], results[1])
        cols = pl.ds(pl.multiple_of(p * 128, 128), 128)
        for b in range(2):
            rows = both[b * BLOCK:(b + 1) * BLOCK].astype(bf16)
            for g in range(G):
                ge = gctx[2 * p].reshape(2 * BLOCK, 128)[g * BLOCK:(g + 1) * BLOCK]
                go = gctx[2 * p + 1].reshape(2 * BLOCK, 128)[g * BLOCK:(g + 1) * BLOCK]
                rows = jnp.where(2 * me + b == gb[g], jnp.where(low_b, ge, go), rows)
            att[b * BLOCK:(b + 1) * BLOCK, cols] = rows
        return c

    def attend_two(i, c):
        return attend(2 * i + 1, attend(2 * i, c))

    lax.fori_loop(0, pairs // 2, attend_two, 0)
    mixed = hidden[...].astype(f32) + jnp.dot(att[...], weight[...], preferred_element_type=f32)
    mean = jnp.mean(mixed, axis=1, keepdims=True)
    centred = mixed - mean
    var = jnp.mean(centred * centred, axis=1, keepdims=True)
    out[...] = (centred * lax.rsqrt(var + 1e-05) * gain[...]).astype(bf16)

    wait_sent(candq.at[pl.ds(0, plane - 1)], 0)
    wait_sent(candkv.at[pl.ds(0, plane - 1)], 1)
    wait_sent(zq.at[pl.ds(0, NZ - 1)], 2)
    wait_sent(gq.at[pl.ds(0, plane - 1)], 3)
    wait_sent(zrkv.at[pl.ds(0, NZ - 1)], 4)
    w0.wait_send()
    w1.wait_send()
    wait_sent(rpart.at[pl.ds(0, plane - 1)], 7)
    wait_sent(gkv.at[pl.ds(0, plane - 1)], 8)
    wait_sent(zpart.at[pl.ds(0, NZ - 1)], 9)
    wait_sent(ghead.at[pl.ds(0, NZ - 1)], 10)
    wait_sent(zkv.at[pl.ds(0, NZ - 1)], 12)
    wait_sent(gctx.at[pl.ds(0, plane - 1)], 11)
    pltpu.make_async_copy(recv.at[pl.ds(0, 2 * count - 2)], recv.at[pl.ds(0, 2 * count - 2)], a2a_s).wait()


def per_device(queries, keys, values, hidden, out_weight, norm_gain, random_blocks, global_blocks):
    row_count, width = queries.shape
    heads, rand = random_blocks.shape[1:]
    count, plane = NX * NY * NZ, NX * NY
    zrows = 2 * BLOCK // NZ
    vmem = pl.BlockSpec(memory_space=pltpu.VMEM)
    smem = pl.BlockSpec(memory_space=pltpu.SMEM)
    shape = jax.ShapeDtypeStruct
    hbm = pl.BlockSpec(memory_space=pltpu.HBM)
    chunk = G * BLOCK // NZ
    tab, rtab = pl.pallas_call(
        functools.partial(table_kernel, heads, rand),
        out_shape=(shape((2, 2 * count), jnp.int32), shape((heads, 128), jnp.int32)),
        in_specs=[vmem],
        out_specs=(smem, smem),
        scratch_shapes=[
            pltpu.VMEM((2, 2 * count), jnp.int32),
            pltpu.VMEM((heads, 128), jnp.int32),
            pltpu.SemaphoreType.DMA((2,)),
        ],
        name="tables",
    )(jnp.transpose(random_blocks, (2, 1, 0)))
    return pl.pallas_call(
        functools.partial(main_kernel, heads, rand),
        out_shape=shape((row_count, width), bf16),
        in_specs=[hbm] * 6 + [smem] * 3,
        out_specs=vmem,
        scratch_shapes=[
            pltpu.VMEM((row_count, width), bf16),
            pltpu.VMEM((row_count, width), bf16),
            pltpu.VMEM((row_count, width), bf16),
            pltpu.VMEM((row_count, width), bf16),
            pltpu.VMEM((width, width), bf16),
            pltpu.VMEM((1, width), f32),
            pltpu.VMEM((2 * count, BLOCK, 128), bf16),
            pltpu.VMEM((2 * heads, BLOCK, 128), bf16),
            pltpu.VMEM((heads, 2 * BLOCK, 128), bf16),
            pltpu.VMEM((heads, BLOCK, 128), bf16),
            pltpu.VMEM((plane, BLOCK, 128), bf16),
            pltpu.VMEM((heads, NZ, chunk, 128), bf16),
            pltpu.VMEM((2 * count, BLOCK, 128), bf16),
            pltpu.VMEM((2, heads, BLOCK, 128), bf16),
            pltpu.VMEM((plane, BLOCK, 128), bf16),
            pltpu.VMEM((NZ, BLOCK, 128), bf16),
            pltpu.VMEM((plane, BLOCK, 128), bf16),
            pltpu.VMEM((plane, NZ, chunk, 128), bf16),
            pltpu.VMEM((NZ, chunk, 128), bf16),
            pltpu.VMEM((NZ, chunk, 128), bf16),
            pltpu.VMEM((NZ, chunk, 128), bf16),
            pltpu.VMEM((plane, NZ, chunk, 128), bf16),
            pltpu.VMEM((heads, 2 * BLOCK, 128), f32),
            pltpu.VMEM((heads, 2 * BLOCK, 128), f32),
            pltpu.VMEM((NZ, zrows, 128), f32),
            pltpu.VMEM((NZ, zrows, 128), f32),
            pltpu.VMEM((NZ, zrows, 128), bf16),
            pltpu.VMEM((heads, NZ, zrows, 128), bf16),
            pltpu.VMEM((row_count, width), bf16),
            pltpu.VMEM((heads, 2 * BLOCK, 6 * BLOCK), f32),
            pltpu.VMEM((heads, 2, 2 * BLOCK, 128), f32),
            pltpu.SemaphoreType.DMA,
            pltpu.SemaphoreType.DMA,
            pltpu.SemaphoreType.DMA((13,)),
            pltpu.SemaphoreType.DMA((13,)),
            pltpu.SemaphoreType.DMA((10,)),
            pltpu.SemaphoreType.DMA((6,)),
        ],
        compiler_params=pltpu.CompilerParams(
            collective_id=0, has_side_effects=True, vmem_limit_bytes=67043328),
        name="main",
    )(queries, keys, values, hidden, out_weight, norm_gain.reshape(1, width),
      global_blocks, tab, rtab)


def solution(mesh):
    placed = (
        P(("dp", "ctx"), None),
        P(("dp", "ctx"), None),
        P(("dp", "ctx"), None),
        P(("dp", "ctx"), None),
        P(),
        P(),
        P("dp", None, None),
        P("dp"),
    )
    return jax.shard_map(
        per_device, mesh=mesh, in_specs=placed, out_specs=P(("dp", "ctx"), None), check_vma=False
    )
```

time: 153 us -> 135 us (0.88)
  Pallas kernels: 144 us -> 133 us
  local copies, waits for them, and re-layouts: 8.88 us -> 1.67 us
    unnamed x19 -> x1, local copies, waits for them, and re-layouts: 8.88 us -> 1.67 us
    pallas_call x1, Pallas kernels: 137 us -> 130 us  [per_device(): pl.pallas_call(functools.partial(main_kernel, heads, rand), out_shape=sha...]
    pallas_call x1, Pallas kernels: 6.68 us -> 2.56 us  [per_device(): pl.pallas_call(functools.partial(table_kernel, heads, rand), out_shape=(s...]
where the time goes in v2:
time: 135 us
  Pallas kernels  133 us (99%)
  local copies, waits for them, and re-layouts  1.67 us (1%)
    pallas_call x1, Pallas kernels, per_device(): pl.pallas_call(functools.partial(main_kernel, heads, rand), out_shape=sha...  130 us

profile of v2, /device:TPU:6, one launch (start us, length us, event | category | flops | bytes accessed | tf_op | source)
XLA Modules:
  0.0 134.5 jit_solution(15170646134811809240)
XLA Ops:
  0.0 2.6 %tables.1 = (s32[2,256]{1,0:T(2,128)}, s32[16,128]{1,0:T(8,128)}) custom-call(s32[3,16,256]{2,1,0:T(8,128)} %bitcast.2), custom_call_target="tpu_custom_call" | custom-call | tf_op jit(solution)/shard_map/tables/pallas_call | solution.py:469
  2.6 130.3 %main.1 = bf16[128,1024]{1,0:T(8,128)(2,1)} custom-call(bf16[128,1024]{1,0:T(8,128)(2,1)} %queries_h.1, bf16[128,1024]{1,0:T(8,128)(2,1)} %keys_h.1, bf16[128,1024]{1,0:T(8,128)(2,1)} %values_h.1, bf16[128,1024]{1,0:T(8,128)(2,1)} %hidden_h.1, bf16[1024,1024]{1,0:T(8,128)(2,1)} %weight_h.1, f32[1,1024]{1,0:T(1,128)} %bitcast.3, s32[2]{0:T(128)} %gb.1, ...), custom_call_target="tpu_custom_call" | custom-call | tf_op jit(solution)/shard_map/main/pallas_call | solution.py:481
  132.9 1.7 %copy.10 = bf16[128,1024]{1,0:T(8,128)(2,1)} copy(bf16[128,1024]{1,0:T(8,128)(2,1)} %main.1) | data formatting | bytes 524288

commit v3 on v2

--- a/solution.py
+++ b/solution.py
@@ -162,6 +162,67 @@
         return c
 
     lax.fori_loop(0, count // 4, fill, 0)
+    pl.semaphore_wait(barrier, count - 1)
+
+    issued = [1]
+
+    def batch(n):
+        lo = issued[0]
+        hi = min(count, lo + n)
+        issued[0] = hi
+
+        def one(k, c):
+            d = shifted((k * 37) % count)
+            remote(payload.at[pl.ds(2 * d, 2)], recv.at[pl.ds(2 * me, 2)], a2a_s, a2a_r, {"ctx": d}).start()
+            return c
+
+        if hi > lo:
+            lax.fori_loop(lo, hi, one, 0)
+
+    def to_plane(fn, i):
+        def one(k, c):
+            p = ((y + k // NX) % NY) * NX + (x + k % NX) % NX
+            src, dst = fn(p)
+            remote(src, dst, send.at[i], got.at[i], at(p % NX, z, p // NX)).start()
+            return c
+
+        lax.fori_loop(1, plane, one, 0)
+
+    def to_line(fn, i):
+        def one(k, c):
+            pz = (z + k) % NZ
+            src, dst = fn(pz)
+            remote(src, dst, send.at[i], got.at[i], at(x, pz, y)).start()
+            return c
+
+        lax.fori_loop(1, NZ, one, 0)
+
+    def wait_got(ref, i):
+        pltpu.make_async_copy(ref, ref, got.at[i]).wait()
+
+    def wait_sent(ref, i):
+        pltpu.make_async_copy(ref, ref, send.at[i]).wait()
+
+    def owner_of(g):
+        return gb[g] // 2
+
+    def pos_of(d):
+        return (d // (NX * NZ)) * NX + d % NX
+
+    def z_of(d):
+        return (d // NX) % NZ
+
+    own = [
+        pltpu.make_async_copy(candq.at[pos], recvq.at[pos], loc.at[0]),
+        pltpu.make_async_copy(candkv.at[pos], recvkv.at[pos], loc.at[1]),
+        pltpu.make_async_copy(payload.at[pl.ds(2 * me, 2)], recv.at[pl.ds(2 * me, 2)], loc.at[2]),
+    ]
+    for c in own:
+        c.start()
+
+    to_plane(lambda p: (candq.at[p], recvq.at[pos]), 0)
+    to_plane(lambda p: (candkv.at[p], recvkv.at[pos]), 1)
+    batch(BATCHES[0])
     zero_b = jnp.zeros((BLOCK, 128), bf16)
     for b in range(2):
         rows = slice(b * BLOCK, (b + 1) * BLOCK)
@@ -169,67 +230,6 @@
             qr = swap_halves(queries[rows, p * 128:(p + 1) * 128])
             qt[2 * p, rows, :] = jnp.where(low_b, zero_b, qr)
             qt[2 * p + 1, rows, :] = jnp.where(low_b, qr, zero_b)
-    pl.semaphore_wait(barrier, count - 1)
-
-    issued = [1]
-
-    def batch(n):
-        lo = issued[0]
-        hi = min(count, lo + n)
-        issued[0] = hi
-
-        def one(k, c):
-            d = shifted((k * 37) % count)
-            remote(payload.at[pl.ds(2 * d, 2)], recv.at[pl.ds(2 * me, 2)], a2a_s, a2a_r, {"ctx": d}).start()
-            return c
-
-        if hi > lo:
-            lax.fori_loop(lo, hi, one, 0)
-
-    def to_plane(fn, i):
-        def one(k, c):
-            p = ((y + k // NX) % NY) * NX + (x + k % NX) % NX
-            src, dst = fn(p)
-            remote(src, dst, send.at[i], got.at[i], at(p % NX, z, p // NX)).start()
-            return c
-
-        lax.fori_loop(1, plane, one, 0)
-
-    def to_line(fn, i):
-        def one(k, c):
-            pz = (z + k) % NZ
-            src, dst = fn(pz)
-            remote(src, dst, send.at[i], got.at[i], at(x, pz, y)).start()
-            return c
-
-        lax.fori_loop(1, NZ, one, 0)
-
-    def wait_got(ref, i):
-        pltpu.make_async_copy(ref, ref, got.at[i]).wait()
-
-    def wait_sent(ref, i):
-        pltpu.make_async_copy(ref, ref, send.at[i]).wait()
-
-    def owner_of(g):
-        return gb[g] // 2
-
-    def pos_of(d):
-        return (d // (NX * NZ)) * NX + d % NX
-
-    def z_of(d):
-        return (d // NX) % NZ
-
-    own = [
-        pltpu.make_async_copy(candq.at[pos], recvq.at[pos], loc.at[0]),
-        pltpu.make_async_copy(candkv.at[pos], recvkv.at[pos], loc.at[1]),
-        pltpu.make_async_copy(payload.at[pl.ds(2 * me, 2)], recv.at[pl.ds(2 * me, 2)], loc.at[2]),
-    ]
-    for c in own:
-        c.start()
-
-    to_plane(lambda p: (candq.at[p], recvq.at[pos]), 0)
-    to_plane(lambda p: (candkv.at[p], recvkv.at[pos]), 1)
-    batch(BATCHES[0])
     own[0].wait()
     wait_got(recvq.at[pl.ds(0, plane - 1)], 0)
     my_g = pos // pairs
@@ -294,7 +294,8 @@
             part[h] = jnp.where(mine, jnp.where(lane % 64 < 32, total, top), numer)
         return c
 
-    lax.fori_loop(0, pairs, partial, 0)
+    for i in range(pairs):
+        partial(i, 0)
     batch(2)
     last_pair = pos // 2
     send_part(2 * last_pair)

time: 135 us -> 136 us (level)
  no operation moved by 1% of the time
where the time goes in v3:
time: 136 us; the launch traced here: 135 us
  Pallas kernels  133 us (98%)
  local copies, waits for them, and re-layouts  1.67 us (1%)
    pallas_call x1, Pallas kernels, per_device(): pl.pallas_call(functools.partial(main_kernel, heads, rand), out_shape=sha...  131 us

profile of v3, /device:TPU:6, one launch (start us, length us, event | category | flops | bytes accessed | tf_op | source)
XLA Modules:
  0.0 134.9 jit_solution(9934015472056614976)
XLA Ops:
  0.0 2.6 %tables.1 = (s32[2,256]{1,0:T(2,128)}, s32[16,128]{1,0:T(8,128)}) custom-call(s32[3,16,256]{2,1,0:T(8,128)} %bitcast.2), custom_call_target="tpu_custom_call" | custom-call | tf_op jit(solution)/shard_map/tables/pallas_call | solution.py:470
  2.6 130.7 %main.1 = bf16[128,1024]{1,0:T(8,128)(2,1)} custom-call(bf16[128,1024]{1,0:T(8,128)(2,1)} %queries_h.1, bf16[128,1024]{1,0:T(8,128)(2,1)} %keys_h.1, bf16[128,1024]{1,0:T(8,128)(2,1)} %values_h.1, bf16[128,1024]{1,0:T(8,128)(2,1)} %hidden_h.1, bf16[1024,1024]{1,0:T(8,128)(2,1)} %weight_h.1, f32[1,1024]{1,0:T(1,128)} %bitcast.3, s32[2]{0:T(128)} %gb.1, ...), custom_call_target="tpu_custom_call" | custom-call | tf_op jit(solution)/shard_map/main/pallas_call | solution.py:482
  133.3 1.7 %copy.10 = bf16[128,1024]{1,0:T(8,128)(2,1)} copy(bf16[128,1024]{1,0:T(8,128)(2,1)} %main.1) | data formatting | bytes 524288
